TPU v7x, 512 devices: a whole 4x8x8 slice. The times are simulated.
512 devices in a mesh: expert: 64 (over z, y), tensor: 8 (over x, core).
Axes of the slice: x: 4, y: 8, z: 8, core: 2. Of those that a mesh axis runs over, the one named last changes fastest.
Arguments:
- tokens: bfloat16 [3072, 4096], P('expert', 'tensor'), may hold values from -6 to 6
- cotangent: bfloat16 [3072, 4096], P('expert', 'tensor'), may hold values from -6 to 6
- expert_ids: int32 [3072, 8], P('expert'), may hold values from 0 to 63, all different within a row; in each aligned block of 48 rows (0 to 47, 48 to 95, ...) at most 8 rows name the same one
- gate_values: float32 [3072, 8], P('expert'), may hold values from 0.05 to 1
- w_gate: bfloat16 [64, 768, 4096], P('expert', 'tensor'), may hold values from -0.09375 to 0.09375
- w_up: bfloat16 [64, 768, 4096], P('expert', 'tensor'), may hold values from -0.09375 to 0.09375
- w_down: bfloat16 [64, 768, 4096], P('expert', 'tensor'), may hold values from -0.21875 to 0.21875
Outputs:
- grad_tokens: bfloat16 [3072, 4096], P('expert', 'tensor')
- grad_gate: bfloat16 [64, 768, 4096], P('expert', 'tensor')
- grad_up: bfloat16 [64, 768, 4096], P('expert', 'tensor')
- grad_down: bfloat16 [64, 768, 4096], P('expert', 'tensor')
Inputs may be any that keep to these rules, and one draw needn't show every extreme that they name: `expert_ids`: each row names 8 different experts. Among the 48 tokens of one index of the expert axis no expert is named more than 8 times, and in every draw some expert is named exactly 8 times there.
All inputs are finite; a program needn't handle non-finite values.
Results may differ from a plain program's by a relative error of at most 0.019.
Values may be sent and summed in bfloat16 or wider, within the bound.
No kernel may reach another device: no remote copies, remote signals or barrier semaphores. Data moves between devices by JAX's collectives and lax.ppermute only.
A program may use at most 64 MiB of HBM per device.

v0:
```python
import jax
import jax.numpy as jnp
from jax import lax
from jax.sharding import PartitionSpec as P

TOP = 8


def expert_backward(rows_x, rows_d, w_gate, w_up, w_down):
    gate_pre = jnp.einsum("secd,ehd->sech", rows_x, w_gate, preferred_element_type=jnp.float32)
    up_pre = jnp.einsum("secd,ehd->sech", rows_x, w_up, preferred_element_type=jnp.float32)
    sigmoid = jax.nn.sigmoid(gate_pre)
    active = gate_pre * sigmoid
    hidden = (active * up_pre).astype(jnp.bfloat16)
    hidden_grad = jnp.einsum("secd,ehd->sech", rows_d, w_down, preferred_element_type=jnp.float32)
    up_grad = (hidden_grad * active).astype(jnp.bfloat16)
    gate_grad = (hidden_grad * up_pre * sigmoid * (1.0 + gate_pre * (1.0 - sigmoid))).astype(
        jnp.bfloat16
    )
    grad_gate = jnp.einsum(
        "sech,secd->ehd", gate_grad, rows_x, preferred_element_type=jnp.float32
    ).astype(jnp.bfloat16)
    grad_up = jnp.einsum(
        "sech,secd->ehd", up_grad, rows_x, preferred_element_type=jnp.float32
    ).astype(jnp.bfloat16)
    grad_down = jnp.einsum(
        "sech,secd->ehd", hidden, rows_d, preferred_element_type=jnp.float32
    ).astype(jnp.bfloat16)
    partial_value = jnp.einsum(
        "sech,ehd->secd", gate_grad, w_gate, preferred_element_type=jnp.float32
    )
    partial_value = partial_value + jnp.einsum(
        "sech,ehd->secd", up_grad, w_up, preferred_element_type=jnp.float32
    )
    return (partial_value, grad_gate, grad_up, grad_down)


def on_device(tokens, cotangent, expert_ids, gate_values, w_gate, w_up, w_down):
    tok_count = expert_ids.shape[0]
    local_count = w_gate.shape[0]
    groups = lax.axis_size("expert")
    experts = local_count * groups
    capacity = 4 * tok_count * TOP // (3 * experts)
    feat_width = tokens.shape[1]
    flat_ids = expert_ids.reshape(-1)
    onehot = (flat_ids[:, None] == jnp.arange(experts, dtype=jnp.int32)[None, :]).astype(jnp.int32)
    before = jnp.cumsum(onehot, axis=0) - onehot
    slot_pos = jnp.sum(before * onehot, axis=1)
    target = flat_ids * capacity + slot_pos
    matches = (target[None, :] == jnp.arange(experts * capacity, dtype=jnp.int32)[:, None]).reshape(
        experts * capacity, tok_count, TOP
    )
    by_token = jnp.any(matches, axis=2)
    occupied = jnp.any(by_token, axis=1)
    token_iota = jnp.arange(tok_count, dtype=jnp.int32)
    owner = jnp.sum(jnp.where(by_token, token_iota[None, :], 0), axis=1)
    slot_weight = jnp.sum(jnp.sum(jnp.where(matches, gate_values[None, :, :], 0.0), axis=2), axis=1)
    full_x, full_d = (
        lax.all_gather(tokens, "tensor", axis=1, tiled=True),
        lax.all_gather(cotangent, "tensor", axis=1, tiled=True),
    )
    sent_x = jnp.where(occupied[:, None], full_x[owner], jnp.zeros((), jnp.bfloat16))
    sent_d = (slot_weight[:, None] * full_d[owner].astype(jnp.float32)).astype(jnp.bfloat16)
    buffer_shape = (groups, local_count, capacity, full_x.shape[1])
    sent_x, sent_d = (sent_x.reshape(buffer_shape), sent_d.reshape(buffer_shape))
    rows_x, rows_d = (
        lax.all_to_all(sent_x, "expert", split_axis=0, concat_axis=0, tiled=True),
        lax.all_to_all(sent_d, "expert", split_axis=0, concat_axis=0, tiled=True),
    )
    partial_value, grad_gate, grad_up, grad_down = expert_backward(
        rows_x, rows_d, w_gate, w_up, w_down
    )
    summed = lax.psum(partial_value.astype(jnp.bfloat16), "tensor").astype(jnp.float32)
    returned = lax.dynamic_slice_in_dim(
        summed, lax.axis_index("tensor") * feat_width, feat_width, 3
    ).astype(jnp.bfloat16)
    arrived = lax.all_to_all(returned, "expert", split_axis=0, concat_axis=0, tiled=True).reshape(
        experts * capacity, feat_width
    )
    masked = jnp.where(occupied[:, None], arrived.astype(jnp.float32), jnp.zeros((), jnp.float32))
    grad_tokens = jax.ops.segment_sum(masked, owner, num_segments=tok_count).astype(jnp.bfloat16)
    return (grad_tokens, grad_gate, grad_up, grad_down)


def solution(mesh):
    return jax.shard_map(
        on_device,
        mesh=mesh,
        in_specs=(
            P("expert", "tensor"),
            P("expert", "tensor"),
            P("expert", None),
            P("expert", None),
            P("expert", "tensor", None),
            P("expert", "tensor", None),
            P("expert", "tensor", None),
        ),
        out_specs=(
            P("expert", "tensor"),
            P("expert", "tensor", None),
            P("expert", "tensor", None),
            P("expert", "tensor", None),
        ),
        check_vma=False,
    )
```

profile of v0, /device:TPU:15, one launch (start us, length us, event | category | flops | bytes accessed | tf_op | source)
XLA Modules:
  0.0 448.9 jit_solution(7881900945583448381)
XLA Ops:
  7.2 0.0 copy-start
  7.2 0.8 copy.49
  8.0 0.1 eq.43
  8.1 0.1 eq.39
  8.2 0.9 reduce-window.6
  9.1 0.2 slice_reduce_fusion
  9.4 0.1 fusion.47
  9.5 0.1 reduce_sum.34
  9.6 0.1 copy.52
  9.7 0.7 multiply_add_fusion
  10.4 0.1 copy.53
  10.5 0.3 fusion.33
  10.9 0.1 broadcast_in_dim.73
  11.0 13.7 %all_gather.7 = bf16[48,4096]{1,0:T(8,128)(2,1)S(1)} all-gather(bf16[48,512]{1,0:T(8,128)(2,1)} %param.7), channel_id=1, replica_groups=mesh['expert'=64,'tensor'=8] {'tensor'}, dimensions={1}, use_global_device_ids=true | all-gather | bytes 442368 | tf_op jit(solution)/shard_map/all_gather | solution.py:59
  24.6 4.3 gather_fusion.1
  29.0 4.5 %bitcast_select_fusion = bf16[64,1,8,4096]{3,2,1,0:T(8,128)(2,1)} fusion(bf16[512,4096]{1,0:T(8,128)(2,1)} %gather_fusion.1, pred[64,8]{1,0:T(8,128)(4,1)S(1)} %broadcast_in_dim.73), kind=kLoop, calls=%fused_computation.16 | loop fusion | flops 2097152 | bytes 8389120 | tf_op jit(solution)/shard_map/jit(_where)/select_n | solution.py:62
  33.5 0.0 copy-start.3
  33.5 0.0 copy-start.2
  33.5 16.3 %all-to-all-start.1 = ((bf16[64,1,8,4096]{3,2,1,0:T(8,128)(2,1)}), bf16[64,1,8,4096]{3,2,1,0:T(8,128)(2,1)}, u32[]{:S(2)}, u32[]{:S(2)}) async-start(bf16[64,1,8,4096]{3,2,1,0:T(8,128)(2,1)} %bitcast_select_fusion), calls=%async_computation.1 | async-start | bytes 8388608 | tf_op jit(solution)/shard_map/all_to_all | solution.py:67
  49.8 0.0 copy-done.3
  49.9 0.1 copy.54
  49.9 0.2 select_reduce_fusion
  50.1 0.1 mul.57
  50.2 0.0 copy-done.2
  50.2 13.5 %all_gather.6 = bf16[48,4096]{1,0:T(8,128)(2,1)S(1)} all-gather(bf16[48,512]{1,0:T(8,128)(2,1)S(1)} %copy-done.2), channel_id=1, replica_groups=mesh['expert'=64,'tensor'=8] {'tensor'}, dimensions={1}, use_global_device_ids=true | all-gather | bytes 442368 | tf_op jit(solution)/shard_map/all_gather | solution.py:60
  63.8 4.4 gather_fusion
  68.1 5.6 %fusion = bf16[64,1,8,4096]{3,2,1,0:T(8,128)(2,1)} fusion(bf16[512,4096]{1,0:T(8,128)(2,1)} %gather_fusion, f32[64,8]{1,0:T(8,128)S(1)} %mul.57), kind=kLoop, calls=%fused_computation.4 | loop fusion | flops 6291456 | bytes 8390656 | tf_op jit(solution)/shard_map/convert_element_type | solution.py:63
  73.8 84.2 %all-to-all-done.1 = bf16[64,1,8,4096]{3,2,1,0:T(8,128)(2,1)} async-done(((bf16[64,1,8,4096]{3,2,1,0:T(8,128)(2,1)}), bf16[64,1,8,4096]{3,2,1,0:T(8,128)(2,1)}, u32[]{:S(2)}, u32[]{:S(2)}) %all-to-all-start.1) | async-done | bytes 4194336 | tf_op jit(solution)/shard_map/all_to_all | solution.py:67
  158.0 33.7 %all-to-all-start = ((bf16[64,1,8,4096]{3,2,1,0:T(8,128)(2,1)}), bf16[64,1,8,4096]{3,2,1,0:T(8,128)(2,1)}, u32[]{:S(2)}, u32[]{:S(2)}) async-start(bf16[64,1,8,4096]{3,2,1,0:T(8,128)(2,1)} %fusion), calls=%async_computation | async-start | bytes 8388608 | tf_op jit(solution)/shard_map/all_to_all | solution.py:68
  191.7 0.0 copy-start.1
  191.7 0.0 copy-start.4
  191.7 0.2 all-reduce.2.cloned.1.call-start
  191.9 0.0 copy-done
  191.9 3.6 fusion.23
  195.5 0.0 copy-done.1
  195.5 3.4 fusion.20
  198.9 105.7 %all-to-all-done = bf16[64,1,8,4096]{3,2,1,0:T(8,128)(2,1)} async-done(((bf16[64,1,8,4096]{3,2,1,0:T(8,128)(2,1)}), bf16[64,1,8,4096]{3,2,1,0:T(8,128)(2,1)}, u32[]{:S(2)}, u32[]{:S(2)}) %all-to-all-start) | async-done | bytes 4194336 | tf_op jit(solution)/shard_map/all_to_all | solution.py:68
  304.6 0.0 copy-done.4
  304.6 3.4 fusion.40
  308.1 1.2 fusion.27
  309.3 3.2 fusion.1
  312.6 0.0 all-reduce.2.cloned.1.call-update
  312.6 91.5 %all-reduce.2.cloned.1.call-done = bf16[64,1,8,4096]{3,2,0,1:T(8,128)(2,1)} async-done(((bf16[64,1,8,4096]{3,2,0,1:T(8,128)(2,1)}), bf16[64,1,8,4096]{3,2,0,1:T(8,128)(2,1)}) %all-reduce.2.cloned.1.call-update) | async-done | bytes 4194320 | tf_op jit(solution)/shard_map/psum | solution.py:73
  404.0 1.9 fusion.35
  405.9 12.8 %all-to-all-start.2 = ((bf16[64,1,8,512]{3,2,1,0:T(8,128)(2,1)}), bf16[64,1,8,512]{3,2,1,0:T(8,128)(2,1)S(1)}, u32[]{:S(2)}, u32[]{:S(2)}) async-start(bf16[64,1,8,512]{3,2,1,0:T(8,128)(2,1)} %fusion.35), calls=%async_computation.2 | async-start | bytes 1048576 | tf_op jit(solution)/shard_map/all_to_all | solution.py:77
  418.8 3.9 fusion.6
  422.7 3.9 fusion.7
  426.6 3.9 fusion.5
  430.6 7.1 %all-to-all-done.2 = bf16[64,1,8,512]{3,2,1,0:T(8,128)(2,1)S(1)} async-done(((bf16[64,1,8,512]{3,2,1,0:T(8,128)(2,1)}), bf16[64,1,8,512]{3,2,1,0:T(8,128)(2,1)S(1)}, u32[]{:S(2)}, u32[]{:S(2)}) %all-to-all-start.2) | async-done | bytes 524320 | tf_op jit(solution)/shard_map/all_to_all | solution.py:77
  437.7 3.8 scatter_custom_fusion
  441.4 0.6 convert_element_type.99
  (5 shorter events, 0.1 us)
Async XLA Ops:
  7.2 184.7 %copy-start = (bf16[1,96,4096]{2,1,0:T(8,128)(2,1)S(1)}, bf16[1,96,4096]{2,1,0:T(8,128)(2,1)}, u32[]{:S(2)}) copy-start(bf16[1,96,4096]{2,1,0:T(8,128)(2,1)} %param.11) | copy-start | bytes 2359300
  33.5 16.4 %copy-start.3 = (f32[48,8]{0,1:T(8,128)S(1)}, f32[48,8]{0,1:T(8,128)}, u32[]{:S(2)}) copy-start(f32[48,8]{0,1:T(8,128)} %param.10) | copy-start | bytes 4612
  33.5 16.7 %copy-start.2 = (bf16[48,512]{1,0:T(8,128)(2,1)S(1)}, bf16[48,512]{1,0:T(8,128)(2,1)}, u32[]{:S(2)}) copy-start(bf16[48,512]{1,0:T(8,128)(2,1)} %param.8) | copy-start | bytes 147460
  33.5 124.5 %all-to-all-start.1 = ((bf16[64,1,8,4096]{3,2,1,0:T(8,128)(2,1)}), bf16[64,1,8,4096]{3,2,1,0:T(8,128)(2,1)}, u32[]{:S(2)}, u32[]{:S(2)}) async-start(bf16[64,1,8,4096]{3,2,1,0:T(8,128)(2,1)} %bitcast_select_fusion), calls=%async_computation.1 | async-start | bytes 8388608 | tf_op jit(solution)/shard_map/all_to_all | solution.py:67
  158.0 146.7 %all-to-all-start = ((bf16[64,1,8,4096]{3,2,1,0:T(8,128)(2,1)}), bf16[64,1,8,4096]{3,2,1,0:T(8,128)(2,1)}, u32[]{:S(2)}, u32[]{:S(2)}) async-start(bf16[64,1,8,4096]{3,2,1,0:T(8,128)(2,1)} %fusion), calls=%async_computation | async-start | bytes 8388608 | tf_op jit(solution)/shard_map/all_to_all | solution.py:68
  191.7 3.8 copy-start.1
  191.7 113.0 %copy-start.4 = (bf16[1,96,4096]{2,1,0:T(8,128)(2,1)S(1)}, bf16[1,96,4096]{2,1,0:T(8,128)(2,1)}, u32[]{:S(2)}) copy-start(bf16[1,96,4096]{2,1,0:T(8,128)(2,1)} %param.13) | copy-start | bytes 2359300
  191.7 212.4 %all-reduce.2.cloned.1.call-start = ((), (), s32[]{:S(2)}) async-start(), calls=%async_computation.3 | async-start | bytes 8388608 | tf_op jit(solution)/shard_map/psum | solution.py:73
  405.9 31.7 %all-to-all-start.2 = ((bf16[64,1,8,512]{3,2,1,0:T(8,128)(2,1)}), bf16[64,1,8,512]{3,2,1,0:T(8,128)(2,1)S(1)}, u32[]{:S(2)}, u32[]{:S(2)}) async-start(bf16[64,1,8,512]{3,2,1,0:T(8,128)(2,1)} %fusion.35), calls=%async_computation.2 | async-start | bytes 1048576 | tf_op jit(solution)/shard_map/all_to_all | solution.py:77
Sparse Core Ops, SparseCore 0:
  312.7 91.2 all-reduce.1
where the time goes:
time: 450 us; the launch traced here: 449 us
  waiting for transfers between devices  288 us (64%)
  starting transfers between devices  63.1 us (14%)
  blocking collectives  27.2 us (6%)
  matrix products  26.7 us (6%)
  other arithmetic  18.7 us (4%)
  between operations  14.2 us (3%)
  local copies, waits for them, and re-layouts  10.5 us (2%)
    all_to_all x1, waiting for transfers between devices, on_device(): lax.all_to_all(sent_d, 'expert', split_axis=0, concat_axis=0, tiled=True)  106 us
    psum x1, waiting for transfers between devices, on_device(): lax.psum(partial_value.astype(jnp.bfloat16), 'tensor').astype(jnp.float32)  91.5 us
    all_to_all x1, waiting for transfers between devices, on_device(): lax.all_to_all(sent_x, 'expert', split_axis=0, concat_axis=0, tiled=True)  84.2 us
    all_to_all x1, starting transfers between devices, on_device(): lax.all_to_all(sent_d, 'expert', split_axis=0, concat_axis=0, tiled=True)  33.7 us
    all_to_all x1, starting transfers between devices, on_device(): lax.all_to_all(sent_x, 'expert', split_axis=0, concat_axis=0, tiled=True)  16.3 us
    all_gather x1, blocking collectives, on_device(): lax.all_gather(tokens, 'tensor', axis=1, tiled=True)  13.7 us
    all_gather x1, blocking collectives, on_device(): lax.all_gather(cotangent, 'tensor', axis=1, tiled=True)  13.5 us
    all_to_all x1, starting transfers between devices, on_device(): lax.all_to_all(returned, 'expert', split_axis=0, concat_axis=0, tiled=True)  12.8 us
  transfers between devices with their start and end apart: 4, of which 4 were waited for; matrix products, arithmetic and copies ran while one was open for 6% of the time, Pallas kernels for 0%

commit v1 on v0

--- a/solution.py
+++ b/solution.py
@@ -70,7 +70,9 @@
     partial_value, grad_gate, grad_up, grad_down = expert_backward(
         rows_x, rows_d, w_gate, w_up, w_down
     )
-    summed = lax.psum(partial_value.astype(jnp.bfloat16), "tensor").astype(jnp.float32)
+    summed = jnp.sum(lax.all_gather(partial_value.astype(jnp.bfloat16), "tensor"), axis=0).astype(
+        jnp.float32
+    )
     returned = lax.dynamic_slice_in_dim(
         summed, lax.axis_index("tensor") * feat_width, feat_width, 3
     ).astype(jnp.bfloat16)

time: 450 us -> 543 us (1.21)
  the two profiles are of different devices: /device:TPU:15 before, /device:TPU:8 now
where the time goes in v1:
time: 543 us
  waiting for transfers between devices  367 us (68%)
  starting transfers between devices  64.8 us (12%)
  other arithmetic  32.7 us (6%)
  matrix products  26.6 us (5%)
  blocking collectives  26.5 us (5%)
  between operations  14.2 us (3%)
  local copies, waits for them, and re-layouts  10.5 us (2%)
    all_gather x1, waiting for transfers between devices, on_device(): lax.all_gather(partial_value.astype(jnp.bfloat16), 'tensor')  170 us
    all_to_all x1, waiting for transfers between devices, on_device(): lax.all_to_all(sent_d, 'expert', split_axis=0, concat_axis=0, tiled=True)  105 us
    all_to_all x1, waiting for transfers between devices, on_device(): lax.all_to_all(sent_x, 'expert', split_axis=0, concat_axis=0, tiled=True)  84.6 us
    all_to_all x1, starting transfers between devices, on_device(): lax.all_to_all(sent_d, 'expert', split_axis=0, concat_axis=0, tiled=True)  34.3 us
    all_to_all x1, starting transfers between devices, on_device(): lax.all_to_all(sent_x, 'expert', split_axis=0, concat_axis=0, tiled=True)  16.9 us
    reduce_sum x1, other arithmetic, on_device(): jnp.sum(lax.all_gather(partial_value.astype(jnp.bfloat16), 'tensor'), axi...  14 us
    all_gather x1, blocking collectives, on_device(): lax.all_gather(tokens, 'tensor', axis=1, tiled=True)  13.5 us
    all_to_all x1, starting transfers between devices, on_device(): lax.all_to_all(returned, 'expert', split_axis=0, concat_axis=0, tiled=True)  13.4 us
  transfers between devices with their start and end apart: 4, of which 4 were waited for; matrix products, arithmetic and copies ran while one was open for 5% of the time, Pallas kernels for 0%

profile of v1, /device:TPU:8, one launch (start us, length us, event | category | flops | bytes accessed | tf_op | source)
XLA Modules:
  0.0 542.6 jit_solution(17989376060599768695)
XLA Ops:
  7.2 0.0 copy-start
  7.2 0.8 copy.49
  8.0 0.1 eq.43
  8.1 0.1 eq.39
  8.2 0.9 reduce-window.6
  9.1 0.2 slice_reduce_fusion
  9.4 0.1 fusion.47
  9.5 0.1 reduce_sum.46
  9.6 0.1 copy.52
  9.7 0.7 multiply_add_fusion
  10.4 0.1 copy.53
  10.5 0.3 fusion.33
  10.9 0.1 broadcast_in_dim.73
  11.0 13.5 %all_gather.13 = bf16[48,4096]{1,0:T(8,128)(2,1)S(1)} all-gather(bf16[48,512]{1,0:T(8,128)(2,1)} %param.7), channel_id=1, replica_groups=mesh['expert'=64,'tensor'=8] {'tensor'}, dimensions={1}, use_global_device_ids=true | all-gather | bytes 442368 | tf_op jit(solution)/shard_map/all_gather | solution.py:59
  24.5 4.4 gather_fusion.1
  28.9 4.5 bitcast_select_fusion
  33.3 0.0 copy-start.3
  33.3 0.0 copy-start.2
  33.3 16.9 %all-to-all-start.1 = ((bf16[64,1,8,4096]{3,2,1,0:T(8,128)(2,1)}), bf16[64,1,8,4096]{3,2,1,0:T(8,128)(2,1)}, u32[]{:S(2)}, u32[]{:S(2)}) async-start(bf16[64,1,8,4096]{3,2,1,0:T(8,128)(2,1)} %bitcast_select_fusion), calls=%async_computation.1 | async-start | bytes 8388608 | tf_op jit(solution)/shard_map/all_to_all | solution.py:67
  50.3 0.0 copy-done.3
  50.3 0.1 copy.54
  50.3 0.2 select_reduce_fusion
  50.5 0.1 mul.57
  50.6 0.0 copy-done.2
  50.6 13.0 %all_gather.12 = bf16[48,4096]{1,0:T(8,128)(2,1)S(1)} all-gather(bf16[48,512]{1,0:T(8,128)(2,1)S(1)} %copy-done.2), channel_id=1, replica_groups=mesh['expert'=64,'tensor'=8] {'tensor'}, dimensions={1}, use_global_device_ids=true | all-gather | bytes 442368 | tf_op jit(solution)/shard_map/all_gather | solution.py:60
  63.6 4.3 gather_fusion
  68.0 5.6 %fusion = bf16[64,1,8,4096]{3,2,1,0:T(8,128)(2,1)} fusion(bf16[512,4096]{1,0:T(8,128)(2,1)} %gather_fusion, f32[64,8]{1,0:T(8,128)S(1)} %mul.57), kind=kLoop, calls=%fused_computation.5 | loop fusion | flops 6291456 | bytes 8390656 | tf_op jit(solution)/shard_map/convert_element_type | solution.py:63
  73.6 84.6 %all-to-all-done.1 = bf16[64,1,8,4096]{3,2,1,0:T(8,128)(2,1)} async-done(((bf16[64,1,8,4096]{3,2,1,0:T(8,128)(2,1)}), bf16[64,1,8,4096]{3,2,1,0:T(8,128)(2,1)}, u32[]{:S(2)}, u32[]{:S(2)}) %all-to-all-start.1) | async-done | bytes 4194336 | tf_op jit(solution)/shard_map/all_to_all | solution.py:67
  158.2 34.3 %all-to-all-start = ((bf16[64,1,8,4096]{3,2,1,0:T(8,128)(2,1)}), bf16[64,1,8,4096]{3,2,1,0:T(8,128)(2,1)}, u32[]{:S(2)}, u32[]{:S(2)}) async-start(bf16[64,1,8,4096]{3,2,1,0:T(8,128)(2,1)} %fusion), calls=%async_computation | async-start | bytes 8388608 | tf_op jit(solution)/shard_map/all_to_all | solution.py:68
  192.5 0.0 copy-start.1
  192.6 0.0 copy-start.4
  192.6 0.2 all-gather.3.cloned.1.call-start
  192.8 0.0 copy-done
  192.8 3.6 fusion.23
  196.4 0.0 copy-done.1
  196.4 3.4 fusion.20
  199.8 105.1 %all-to-all-done = bf16[64,1,8,4096]{3,2,1,0:T(8,128)(2,1)} async-done(((bf16[64,1,8,4096]{3,2,1,0:T(8,128)(2,1)}), bf16[64,1,8,4096]{3,2,1,0:T(8,128)(2,1)}, u32[]{:S(2)}, u32[]{:S(2)}) %all-to-all-start) | async-done | bytes 4194336 | tf_op jit(solution)/shard_map/all_to_all | solution.py:68
  304.9 0.0 copy-done.4
  304.9 3.4 fusion.40
  308.3 1.2 fusion.27
  309.6 3.2 fusion.1
  312.7 0.0 all-gather.3.cloned.1.call-update
  312.8 169.7 %all-gather.3.cloned.1.call-done = bf16[512,1,8,4096]{3,2,1,0:T(8,128)(2,1)} async-done(((bf16[64,1,8,4096]{3,2,1,0:T(8,128)(2,1)}), bf16[512,1,8,4096]{3,2,1,0:T(8,128)(2,1)}) %all-gather.3.cloned.1.call-update) | async-done | bytes 33554448 | tf_op jit(solution)/shard_map/all_gather | solution.py:73
  482.5 14.0 %bitcast_reduce_fusion = bf16[64,8,4096]{2,1,0:T(8,128)(2,1)} fusion(bf16[8,64,8,4096]{3,2,1,0:T(8,128)(2,1)} %bitcast.147), kind=kLoop, calls=%fused_computation.3 | loop fusion | flops 14680064 | bytes 37748736 | tf_op jit(solution)/shard_map/reduce_sum | solution.py:73
  496.5 1.9 fusion.35
  498.4 13.4 %all-to-all-start.2 = ((bf16[64,1,8,512]{3,2,1,0:T(8,128)(2,1)}), bf16[64,1,8,512]{3,2,1,0:T(8,128)(2,1)S(1)}, u32[]{:S(2)}, u32[]{:S(2)}) async-start(bf16[64,1,8,512]{3,2,1,0:T(8,128)(2,1)} %fusion.35), calls=%async_computation.2 | async-start | bytes 1048576 | tf_op jit(solution)/shard_map/all_to_all | solution.py:79
  511.8 3.9 fusion.6
  515.7 3.9 fusion.7
  519.6 3.9 fusion.5
  523.6 7.9 %all-to-all-done.2 = bf16[64,1,8,512]{3,2,1,0:T(8,128)(2,1)S(1)} async-done(((bf16[64,1,8,512]{3,2,1,0:T(8,128)(2,1)}), bf16[64,1,8,512]{3,2,1,0:T(8,128)(2,1)S(1)}, u32[]{:S(2)}, u32[]{:S(2)}) %all-to-all-start.2) | async-done | bytes 524320 | tf_op jit(solution)/shard_map/all_to_all | solution.py:79
  531.4 3.8 scatter_custom_fusion
  535.2 0.6 convert_element_type.114
  (5 shorter events, 0.1 us)
Async XLA Ops:
  7.2 185.6 %copy-start = (bf16[1,96,4096]{2,1,0:T(8,128)(2,1)S(1)}, bf16[1,96,4096]{2,1,0:T(8,128)(2,1)}, u32[]{:S(2)}) copy-start(bf16[1,96,4096]{2,1,0:T(8,128)(2,1)} %param.11) | copy-start | bytes 2359300
  33.3 16.9 %copy-start.3 = (f32[48,8]{0,1:T(8,128)S(1)}, f32[48,8]{0,1:T(8,128)}, u32[]{:S(2)}) copy-start(f32[48,8]{0,1:T(8,128)} %param.10) | copy-start | bytes 4612
  33.3 17.3 %copy-start.2 = (bf16[48,512]{1,0:T(8,128)(2,1)S(1)}, bf16[48,512]{1,0:T(8,128)(2,1)}, u32[]{:S(2)}) copy-start(bf16[48,512]{1,0:T(8,128)(2,1)} %param.8) | copy-start | bytes 147460
  33.3 124.9 %all-to-all-start.1 = ((bf16[64,1,8,4096]{3,2,1,0:T(8,128)(2,1)}), bf16[64,1,8,4096]{3,2,1,0:T(8,128)(2,1)}, u32[]{:S(2)}, u32[]{:S(2)}) async-start(bf16[64,1,8,4096]{3,2,1,0:T(8,128)(2,1)} %bitcast_select_fusion), calls=%async_computation.1 | async-start | bytes 8388608 | tf_op jit(solution)/shard_map/all_to_all | solution.py:67
  158.2 146.7 %all-to-all-start = ((bf16[64,1,8,4096]{3,2,1,0:T(8,128)(2,1)}), bf16[64,1,8,4096]{3,2,1,0:T(8,128)(2,1)}, u32[]{:S(2)}, u32[]{:S(2)}) async-start(bf16[64,1,8,4096]{3,2,1,0:T(8,128)(2,1)} %fusion), calls=%async_computation | async-start | bytes 8388608 | tf_op jit(solution)/shard_map/all_to_all | solution.py:68
  192.5 3.8 copy-start.1
  192.6 112.3 %copy-start.4 = (bf16[1,96,4096]{2,1,0:T(8,128)(2,1)S(1)}, bf16[1,96,4096]{2,1,0:T(8,128)(2,1)}, u32[]{:S(2)}) copy-start(bf16[1,96,4096]{2,1,0:T(8,128)(2,1)} %param.13) | copy-start | bytes 2359300
  192.6 289.9 %all-gather.3.cloned.1.call-start = ((), (), s32[]{:S(2)}) async-start(), calls=%async_computation.3 | async-start | bytes 37748736 | tf_op jit(solution)/shard_map/all_gather | solution.py:73
  498.4 33.0 %all-to-all-start.2 = ((bf16[64,1,8,512]{3,2,1,0:T(8,128)(2,1)}), bf16[64,1,8,512]{3,2,1,0:T(8,128)(2,1)S(1)}, u32[]{:S(2)}, u32[]{:S(2)}) async-start(bf16[64,1,8,512]{3,2,1,0:T(8,128)(2,1)} %fusion.35), calls=%async_computation.2 | async-start | bytes 1048576 | tf_op jit(solution)/shard_map/all_to_all | solution.py:79
Sparse Core Ops, SparseCore 0:
  312.9 169.5 all-gather.2
